TPU v7x, 32 devices: a whole 2x2x4 slice. The times are simulated.
32 devices in a mesh: grp: 4 (over x, core), blk: 8 (over z, y).
Axes of the slice: x: 2, y: 2, z: 4, core: 2. Of those that a mesh axis runs over, the one named last changes fastest.
Arguments:
- masses: bfloat16 [8, 2, 256, 256], P('blk'), may hold values from -3 to 3
- spins: int32 [8, 256], P('blk'), may hold values from 0 to 1
- shift_table: int32 [32, 256], P('blk'), may hold values from 0 to 255, as said below
- flip_table: int32 [32, 256], P('blk'), may hold values from 0 to 255, as said below
- ph_in: float32 [2, 32, 256, 256], P(None, 'blk', 'grp'), may hold values from -6 to 6
- pp_in: float32 [2, 32, 256, 256], P(None, 'blk', 'grp'), may hold values from -6 to 6
Outputs:
- ph_out: float32 [2, 32, 256, 256], P(None, 'blk', 'grp')
- pp_out: float32 [2, 32, 256, 256], P(None, 'blk', 'grp')
Inputs may be any that keep to these rules, and one draw needn't show every extreme that they name: Row t of shift_table maps w * 16 + k to ((w + n_t) mod 16) * 16 + (k + q_t) mod 16 for some integers n_t, q_t of the transfer; every row is a permutation. Row t of flip_table maps w * 16 + k to ((n_t - w - 1) mod 16) * 16 + (q_t - k) mod 16 with the same n_t, q_t as shift_table's row t.
All inputs are finite; a program needn't handle non-finite values.
Results may differ from a plain program's by a relative error of at most 0.0064.
Values may be sent and summed in bfloat16 or wider, within the bound.
A program may use at most 128 MiB of HBM per device.

v0:
```python
import math

import jax
import jax.numpy as jnp
from jax import lax
from jax.sharding import PartitionSpec as P

NW = 16
NK = 16


COUPLING = 0.5


def shifted(value, axis, steps):
    count = lax.axis_size(axis)
    pairs = [(source, (source + steps) % count) for source in range(count)]
    return lax.ppermute(value, axis, pairs)


def dft_tables():
    index = jnp.arange(NW * NK, dtype=jnp.int32)
    frequency = index // NK
    momentum = index % NK
    numerator = (
        (2 * frequency[:, None] + 1) * frequency[None, :] * NK
        - 2 * momentum[:, None] * momentum[None, :] * NW
    ) % (2 * NW * NK)
    phase = numerator.astype(jnp.float32) * (math.pi / (NW * NK))
    norm_scale = 1.0 / math.sqrt(NW * NK)
    return (
        (jnp.cos(phase) * norm_scale).astype(jnp.bfloat16),
        (jnp.sin(phase) * norm_scale).astype(jnp.bfloat16),
    )


def build_band(masses, spins, rows_real, rows_imag, real_table, imag_table):
    signed = (2 * spins - 1).astype(jnp.float32)
    factors = jnp.stack([jnp.exp(COUPLING * signed), jnp.exp(-COUPLING * signed)], 1)
    scaled = (masses.astype(jnp.float32) * factors[:, :, None, :]).astype(jnp.bfloat16)
    first_real = jnp.einsum(
        "ri,wsij->wsrj", rows_real, scaled, preferred_element_type=jnp.float32
    ).astype(jnp.bfloat16)
    first_imag = jnp.einsum(
        "ri,wsij->wsrj", rows_imag, scaled, preferred_element_type=jnp.float32
    ).astype(jnp.bfloat16)
    joined = jnp.concatenate([first_real, first_imag], -1)
    big_table = jnp.concatenate(
        [
            jnp.concatenate([real_table.T, -imag_table.T], 1),
            jnp.concatenate([imag_table.T, real_table.T], 1),
        ],
        0,
    )
    second = jnp.einsum("wsri,ij->wsrj", joined, big_table, preferred_element_type=jnp.float32)
    order = real_table.shape[1]
    return jnp.stack([second[..., :order], second[..., order:]], 2).astype(jnp.bfloat16)


def window_walkers(payload):
    reach = min(8, lax.axis_size("blk") - 1)
    visits = [payload]
    current = payload
    for offset in range(1, reach + 1):
        current = shifted(current, "blk", 1)
        visits.append(current)
    return visits


def cyclic_window(grid, start, length, axis):
    doubled = jnp.concatenate([grid, grid], axis)
    return lax.dynamic_slice_in_dim(doubled, start, length, axis)


def moved_band(view, freq_move, mom_move, first_freq, band_freq):
    rank = view.ndim
    result = cyclic_window(view, mom_move, NK, rank - 1)
    result = cyclic_window(result, freq_move, NW, rank - 2)
    result = cyclic_window(result, mom_move, NK, rank - 3)
    result = cyclic_window(result, first_freq + freq_move, band_freq, rank - 4)
    lead = view.shape[: rank - 4]
    return result.reshape(lead + (band_freq * NK, NW * NK))


def absorb(increment, full, first_row, height, shift_starts, flip_starts):
    band_freq = height // NK
    first_freq = first_row // NK
    propagator = full[0]
    columns = lax.dynamic_slice_in_dim(propagator, first_row, height, 3)
    mirrored = jnp.swapaxes(columns, 2, 3).astype(jnp.float32)
    upper = lax.dynamic_slice_in_dim(propagator[0], first_row, height, 1).astype(jnp.float32)
    view = propagator.reshape(2, 2, NW, NK, NW, NK)
    reversed_lower = view[1, :, ::-1, ::-1, ::-1, ::-1]

    def one_transfer(starts):
        shift_start, flip_start = starts
        shift_freq = shift_start // NK
        shift_mom = shift_start % NK
        flip_freq = (NW - 1 - flip_start // NK) % NW
        flip_mom = (NK - 1 - flip_start % NK) % NK
        moved = moved_band(view, shift_freq, shift_mom, first_freq, band_freq).astype(jnp.float32)
        ph_real = jnp.sum(mirrored[:, 0] * moved[:, 0] - mirrored[:, 1] * moved[:, 1], axis=0)
        ph_imag = jnp.sum(mirrored[:, 0] * moved[:, 1] + mirrored[:, 1] * moved[:, 0], axis=0)
        lowered = moved_band(reversed_lower, flip_freq, flip_mom, first_freq, band_freq).astype(
            jnp.float32
        )
        pp_real = upper[0] * lowered[0] - upper[1] * lowered[1]
        pp_imag = upper[0] * lowered[1] + upper[1] * lowered[0]
        return (jnp.stack([ph_real, ph_imag]), jnp.stack([pp_real, pp_imag]))

    ph_step, pp_step = lax.map(one_transfer, (shift_starts, flip_starts))
    increment = (increment[0] + ph_step, increment[1] + pp_step)
    return increment


def on_device(masses, spins, shift_table, flip_table, ph_in, pp_in):
    groups = lax.axis_size("grp")
    order = masses.shape[-1]
    height = order // groups
    first_row = lax.axis_index("grp") * height
    real_table, imag_table = dft_tables()
    shift_starts = shift_table[:, 0]
    flip_starts = flip_table[:, 0]
    trans_count = shift_table.shape[0]
    empty = jnp.zeros((trans_count, 2, height, order), jnp.float32)
    increment = (empty, empty)
    whole = build_band(masses, spins, real_table, imag_table, real_table, imag_table)
    for visit in window_walkers(whole):
        increment = absorb(increment, visit, first_row, height, shift_starts, flip_starts)
    return (ph_in + jnp.swapaxes(increment[0], 0, 1), pp_in + jnp.swapaxes(increment[1], 0, 1))


def solution(mesh):
    placed = (
        P("blk", None, None, None),
        P("blk", None),
        P("blk", None),
        P("blk", None),
        P(None, "blk", "grp", None),
        P(None, "blk", "grp", None),
    )
    return jax.shard_map(
        on_device,
        mesh=mesh,
        in_specs=placed,
        out_specs=(P(None, "blk", "grp", None), P(None, "blk", "grp", None)),
        check_vma=False,
    )
```

profile of v0, /device:TPU:1, one launch (start us, length us, event | category | flops | bytes accessed | tf_op | source)
XLA Modules:
  0.0 1097.4 jit_solution(46076599027587606)
XLA Ops:
  23.0 4.9 pad_maximum_fusion.7
  28.0 6.3 maximum_maximum_fusion
  36.9 99.3 %while.120 = (s32[]{:T(128)}, f32[4,2,64,256]{3,2,0,1:T(8,128)}, f32[4,2,64,256]{3,2,0,1:T(8,128)}, f32[2,2,64,256]{3,2,1,0:T(8,128)S(1)}, s32[4]{0:T(128)S(1)},...) while((s32[]{:T(128)}, f32[4,2,64,256]{3,2,0,1:T(8,128)}, ...), condition=%wide.region_3.4_spmd, body=%wide.region_0.3_spmd.sunk | while | flops 2555988 | bytes 8520749 | solution.py:111
  140.7 17.1 %pad_maximum_fusion = bf16[2,2,16,16,16,32]{5,4,3,2,0,1:T(8,128)(2,1)} fusion(bf16[2,2,16,16,16,16]{5,4,3,2,0,1:T(8,128)(2,1)} %reshape_squeeze.22), kind=kLoop, calls=%fused_computation.241 | loop fusion | flops 2097152 | bytes 1572864 | tf_op jit(solution)/shard_map/while/body/eval_jaxpr/concatenate | solution.py:71
  170.9 109.5 %while.121 = (s32[]{:T(128)}, f32[4,2,64,256]{3,2,0,1:T(8,128)}, f32[4,2,64,256]{3,2,0,1:T(8,128)}, f32[2,2,64,256]{3,2,1,0:T(8,128)S(1)}, s32[4]{0:T(128)S(1)},...) while((s32[]{:T(128)}, f32[4,2,64,256]{3,2,0,1:T(8,128)}, ...), condition=%wide.region_7.8_spmd, body=%wide.region_4.7_spmd.sunk | while | flops 3342420 | bytes 7472173 | solution.py:111
  177.5 8.9 fusion.246
  204.9 8.8 fusion.246
  232.2 8.9 fusion.246
  259.6 8.9 fusion.246
  281.6 5.4 reshape_squeeze.23
  287.0 7.3 pad_maximum_fusion.1
  308.5 109.4 %while.122 = (s32[]{:T(128)}, f32[4,2,64,256]{3,2,0,1:T(8,128)}, f32[4,2,64,256]{3,2,0,1:T(8,128)}, f32[2,2,64,256]{3,2,1,0:T(8,128)S(1)}, s32[4]{0:T(128)S(1)},...) while((s32[]{:T(128)}, f32[4,2,64,256]{3,2,0,1:T(8,128)}, ...), condition=%wide.region_11.12_spmd, body=%wide.region_8.11_spmd.sunk | while | flops 3342420 | bytes 7472173 | solution.py:111
  315.1 8.9 fusion.255
  342.5 8.8 fusion.255
  369.8 8.9 fusion.255
  397.2 8.9 fusion.255
  422.4 7.1 pad_maximum_fusion.2
  442.5 109.4 %while.123 = (s32[]{:T(128)}, f32[4,2,64,256]{3,2,0,1:T(8,128)}, f32[4,2,64,256]{3,2,0,1:T(8,128)}, f32[2,2,64,256]{3,2,1,0:T(8,128)S(1)}, s32[4]{0:T(128)S(1)},...) while((s32[]{:T(128)}, f32[4,2,64,256]{3,2,0,1:T(8,128)}, ...), condition=%wide.region_15.16_spmd, body=%wide.region_12.15_spmd.sunk | while | flops 3342420 | bytes 7472173 | solution.py:111
  449.2 8.9 fusion.264
  476.6 8.8 fusion.264
  503.9 8.9 fusion.264
  531.2 8.9 fusion.264
  553.2 5.4 reshape_squeeze.25
  558.6 7.3 pad_maximum_fusion.3
  580.0 109.4 %while.124 = (s32[]{:T(128)}, f32[4,2,64,256]{3,2,0,1:T(8,128)}, f32[4,2,64,256]{3,2,0,1:T(8,128)}, f32[2,2,64,256]{3,2,1,0:T(8,128)S(1)}, s32[4]{0:T(128)S(1)},...) while((s32[]{:T(128)}, f32[4,2,64,256]{3,2,0,1:T(8,128)}, ...), condition=%wide.region_19.20_spmd, body=%wide.region_16.19_spmd.sunk | while | flops 3342420 | bytes 7472173 | solution.py:111
  586.7 8.9 fusion.273
  614.1 8.8 fusion.273
  641.4 8.9 fusion.273
  668.8 8.9 fusion.273
  694.0 7.1 pad_maximum_fusion.4
  714.2 109.4 %while.125 = (s32[]{:T(128)}, f32[4,2,64,256]{3,2,0,1:T(8,128)}, f32[4,2,64,256]{3,2,0,1:T(8,128)}, f32[2,2,64,256]{3,2,1,0:T(8,128)S(1)}, s32[4]{0:T(128)S(1)},...) while((s32[]{:T(128)}, f32[4,2,64,256]{3,2,0,1:T(8,128)}, ...), condition=%wide.region_23.24_spmd, body=%wide.region_20.23_spmd.sunk | while | flops 3342420 | bytes 7472173 | solution.py:111
  720.9 8.9 fusion.282
  748.2 8.8 fusion.282
  775.6 8.9 fusion.282
  802.9 8.9 fusion.282
  824.9 5.4 reshape_squeeze.27
  830.3 7.3 pad_maximum_fusion.5
  851.8 109.4 %while.126 = (s32[]{:T(128)}, f32[4,2,64,256]{3,2,0,1:T(8,128)}, f32[4,2,64,256]{3,2,0,1:T(8,128)}, f32[2,2,64,256]{3,2,1,0:T(8,128)S(1)}, s32[4]{0:T(128)S(1)},...) while((s32[]{:T(128)}, f32[4,2,64,256]{3,2,0,1:T(8,128)}, ...), condition=%wide.region_27.28_spmd, body=%wide.region_24.27_spmd.sunk | while | flops 3342420 | bytes 7472173 | solution.py:111
  858.5 8.9 fusion.291
  885.8 8.8 fusion.291
  913.1 8.9 fusion.291
  940.5 8.9 fusion.291
  965.8 7.1 pad_maximum_fusion.6
  983.8 108.7 %while.127 = (s32[]{:T(128)}, f32[4,2,64,256]{3,2,0,1:T(8,128)S(1)}, f32[4,2,64,256]{3,2,0,1:T(8,128)}, f32[2,2,64,256]{3,2,1,0:T(8,128)S(1)}, s32[4]{0:T(128)S(...) while((s32[]{:T(128)}, f32[4,2,64,256]{3,2,0,1:T(8,128)S(1)}, ...), condition=%wide.region_31.32_spmd, body=%wide.region_28.31_spmd.sunk | while | flops 3342420 | bytes 7472173 | solution.py:111
  990.4 8.9 fusion.300
  1017.6 8.8 fusion.300
  1044.7 8.9 fusion.300
  1072.0 8.9 fusion.300
  (617 shorter events, 588.8 us)
Async XLA Ops:
  9.7 126.4 %collective-permute-start = (bf16[1,2,2,256,256]{4,3,1,2,0:T(8,128)(2,1)}, bf16[1,2,2,256,256]{4,3,1,2,0:T(8,128)(2,1)S(1)}, u32[]{:S(2)}, u32[]{:S(2)}) collective-permute-start(bf16[1,2,2,256,256]{4,3,1,2,0:T(8,128)(2,1)} %pad_maximum_fusion.15), channel_id=1, source_target_pairs={{0,1},{1,2},{2,3},{3,4},{4,5},{5,6},{6,7},{7,0},{8,9},{9,10},{10,1... | collective-permute-start | bytes 1572872 | tf_op jit(solution)/shard_map/ppermute | solution.py:18
  19.1 8.7 copy-start.10
  19.2 8.7 copy-start.11
  23.0 5.1 copy-start
  167.9 112.4 %collective-permute-start.1 = (bf16[1,2,2,256,256]{4,3,1,2,0:T(8,128)(2,1)S(1)}, bf16[1,2,2,256,256]{4,3,1,2,0:T(8,128)(2,1)}, u32[]{:S(2)}, u32[]{:S(2)}) collective-permute-start(bf16[1,2,2,256,256]{4,3,1,2,0:T(8,128)(2,1)S(1)} %collective-permute-done), channel_id=1, source_target_pairs={{0,1},{1,2},{2,3},{3,4},{4,5},{5,6},{6,7},{7,0},{8,9},{9,10},{10,1... | collective-permute-start | bytes 1572872 | tf_op jit(solution)/shard_map/ppermute | solution.py:18
  305.5 112.4 %collective-permute-start.2 = (bf16[1,2,2,256,256]{4,3,1,2,0:T(8,128)(2,1)}, bf16[1,2,2,256,256]{4,3,1,2,0:T(8,128)(2,1)S(1)}, u32[]{:S(2)}, u32[]{:S(2)}) collective-permute-start(bf16[1,2,2,256,256]{4,3,1,2,0:T(8,128)(2,1)} %collective-permute-done.1), channel_id=1, source_target_pairs={{0,1},{1,2},{2,3},{3,4},{4,5},{5,6},{6,7},{7,0},{8,9},{9,10},{10,1... | collective-permute-start | bytes 1572872 | tf_op jit(solution)/shard_map/ppermute | solution.py:18
  439.6 112.3 %collective-permute-start.3 = (bf16[1,2,2,256,256]{4,3,1,2,0:T(8,128)(2,1)S(1)}, bf16[1,2,2,256,256]{4,3,1,2,0:T(8,128)(2,1)}, u32[]{:S(2)}, u32[]{:S(2)}) collective-permute-start(bf16[1,2,2,256,256]{4,3,1,2,0:T(8,128)(2,1)S(1)} %collective-permute-done.2), channel_id=1, source_target_pairs={{0,1},{1,2},{2,3},{3,4},{4,5},{5,6},{6,7},{7,0},{8,9},{9,10},{10,1... | collective-permute-start | bytes 1572872 | tf_op jit(solution)/shard_map/ppermute | solution.py:18
  577.1 112.4 %collective-permute-start.4 = (bf16[1,2,2,256,256]{4,3,1,2,0:T(8,128)(2,1)}, bf16[1,2,2,256,256]{4,3,1,2,0:T(8,128)(2,1)S(1)}, u32[]{:S(2)}, u32[]{:S(2)}) collective-permute-start(bf16[1,2,2,256,256]{4,3,1,2,0:T(8,128)(2,1)} %collective-permute-done.3), channel_id=1, source_target_pairs={{0,1},{1,2},{2,3},{3,4},{4,5},{5,6},{6,7},{7,0},{8,9},{9,10},{10,1... | collective-permute-start | bytes 1572872 | tf_op jit(solution)/shard_map/ppermute | solution.py:18
  711.2 112.4 %collective-permute-start.5 = (bf16[1,2,2,256,256]{4,3,1,2,0:T(8,128)(2,1)S(1)}, bf16[1,2,2,256,256]{4,3,1,2,0:T(8,128)(2,1)}, u32[]{:S(2)}, u32[]{:S(2)}) collective-permute-start(bf16[1,2,2,256,256]{4,3,1,2,0:T(8,128)(2,1)S(1)} %collective-permute-done.4), channel_id=1, source_target_pairs={{0,1},{1,2},{2,3},{3,4},{4,5},{5,6},{6,7},{7,0},{8,9},{9,10},{10,1... | collective-permute-start | bytes 1572872 | tf_op jit(solution)/shard_map/ppermute | solution.py:18
  848.8 112.5 %collective-permute-start.6 = (bf16[1,2,2,256,256]{4,3,1,2,0:T(8,128)(2,1)}, bf16[1,2,2,256,256]{4,3,1,2,0:T(8,128)(2,1)S(1)}, u32[]{:S(2)}, u32[]{:S(2)}) collective-permute-start(bf16[1,2,2,256,256]{4,3,1,2,0:T(8,128)(2,1)} %collective-permute-done.5), channel_id=1, source_target_pairs={{0,1},{1,2},{2,3},{3,4},{4,5},{5,6},{6,7},{7,0},{8,9},{9,10},{10,1... | collective-permute-start | bytes 1572872 | tf_op jit(solution)/shard_map/ppermute | solution.py:18
  1092.5 3.5 copy-start.1
  1092.5 3.5 copy-start.2
  1092.5 3.5 copy-start.3
  1092.6 3.5 copy-start.4
  1092.6 3.5 copy-start.5
  1092.6 3.5 copy-start.6
  1092.6 3.5 copy-start.7
  1092.6 3.5 copy-start.8
  1092.6 3.5 copy-start.9
where the time goes:
time: 1110 us; the launch traced here: 1100 us
  other arithmetic  544 us (49%)
  local copies, waits for them, and re-layouts  366 us (33%)
  loops' own time  171 us (15%)
    concatenate x116, other arithmetic, cyclic_window(): doubled = jnp.concatenate([grid, grid], axis)  476 us
    dynamic_slice x64, local copies, waits for them, and re-layouts, cyclic_window(): return lax.dynamic_slice_in_dim(doubled, start, length, axis)  182 us
    another operation x8, loops' own time, absorb(): ph_step, pp_step = lax.map(one_transfer, (shift_starts, flip_starts))  171 us
    dynamic_slice x64, local copies, waits for them, and re-layouts, absorb(): ph_step, pp_step = lax.map(one_transfer, (shift_starts, flip_starts))  37.6 us
    another operation x7, local copies, waits for them, and re-layouts, absorb(): view = propagator.reshape(2, 2, NW, NK, NW, NK)  33 us
    rev x8, local copies, waits for them, and re-layouts, absorb(): reversed_lower = view[1, :, ::-1, ::-1, ::-1, ::-1]  30.7 us
    convert_element_type x32, local copies, waits for them, and re-layouts, one_transfer(): moved_band(view, shift_freq, shift_mom, first_freq, band_freq)  30 us
    dynamic_update_slice x32, other arithmetic, absorb(): ph_step, pp_step = lax.map(one_transfer, (shift_starts, flip_starts))  23 us
  transfers between devices with their start and end apart: 7, of which 0 were waited for; matrix products, arithmetic and copies ran while one was open for 58% of the time, Pallas kernels for 0%

commit v1 on v0

v1 whole, which is shorter than its diff:
```python
import functools
import math

import jax
import jax.numpy as jnp
from jax import lax
from jax.experimental import pallas as pl
from jax.experimental.pallas import tpu as pltpu
from jax.sharding import PartitionSpec as P

NW = 16
NK = 16
COUPLING = 0.5
MESH = pl.DeviceIdType.MESH
NT = (((1,), (1,)), ((), ()))


def angle(steps):
    return steps.astype(jnp.float32) * (math.pi / NW)


def base_steps(row, col):
    return ((2 * (row // NK) + 1) * (col // NK) - 2 * (row % NK) * (col % NK)) % (2 * NW)


def move_steps(freq, mom, col):
    return (2 * freq * (col // NK) - 2 * mom * (col % NK)) % (2 * NW)


def kernel(
    blocks, groups, reach, shift_ref, masses_ref, spins_ref, ph_ref, pp_ref, ph_out, pp_out,
    held, held_spins, col_table, sh_cols, fl_cols, band, sh_rows, fl_rows,
    x_ph, x_pp, fixed, recv_sem, spin_recv, direct_sem, spin_send, core_sem, far_sem, relay_sem,
    local_sem,
):
    group = lax.axis_index("grp")
    block = lax.axis_index("blk")
    order = held.shape[-1]
    walkers = held.shape[1]
    trans = ph_out.shape[1]
    height = order // groups
    chips = groups // 2
    chip, core = group // 2, group % 2
    partner = chip * 2 + (1 - core)
    f32, bf16 = jnp.float32, jnp.bfloat16

    def far(step):
        return lax.rem(chip + step, chips) * 2 + core

    def rows_of(piece):
        return pl.ds(pl.multiple_of(piece * height, height), height)

    barrier = pltpu.get_barrier_semaphore()
    for offset in range(1, reach + 1):
        source = lax.rem(block - offset + blocks, blocks)
        pl.semaphore_signal(barrier, inc=1, device_id=(group, source), device_id_type=MESH)
    pl.semaphore_signal(barrier, inc=1, device_id=(partner, block), device_id_type=MESH)
    for step in range(1, chips):
        pl.semaphore_signal(barrier, inc=1, device_id=(far(step), block), device_id_type=MESH)

    local = [
        pltpu.make_async_copy(masses_ref, held.at[0], local_sem.at[0]),
        pltpu.make_async_copy(spins_ref, held_spins.at[0], local_sem.at[1]),
        pltpu.make_async_copy(ph_ref, ph_out, local_sem.at[2]),
        pltpu.make_async_copy(pp_ref, pp_out, local_sem.at[3]),
    ]
    for copy in local:
        copy.start()
    pl.semaphore_wait(barrier, reach + chips)

    def direct(offset):
        target = (group, lax.rem(block + offset, blocks))
        return (
            pltpu.make_async_remote_copy(
                src_ref=masses_ref.at[:, :, rows_of(group)],
                dst_ref=held.at[offset, :, :, rows_of(group)],
                send_sem=direct_sem.at[offset],
                recv_sem=recv_sem.at[offset, group],
                device_id=target,
                device_id_type=MESH,
            ),
            pltpu.make_async_remote_copy(
                src_ref=spins_ref,
                dst_ref=held_spins.at[offset],
                send_sem=spin_send.at[offset],
                recv_sem=spin_recv.at[offset],
                device_id=target,
                device_id_type=MESH,
            ),
        )

    def passed(offset, piece, target, send_sem):
        view = held.at[offset, :, :, rows_of(piece)]
        return pltpu.make_async_remote_copy(
            src_ref=view,
            dst_ref=view,
            send_sem=send_sem,
            recv_sem=recv_sem.at[offset, piece],
            device_id=(target, block),
            device_id_type=MESH,
        )

    def to_core(offset):
        return passed(offset, group, partner, core_sem.at[offset])

    def to_far(offset, step):
        return passed(offset, group, far(step), far_sem.at[step, offset])

    def relay(offset, step):
        return passed(offset, far(step), partner, relay_sem.at[step, offset])

    def arrival(offset, piece):
        return passed(offset, piece, partner, core_sem.at[offset])

    for offset in range(1, reach + 1):
        for copy in direct(offset):
            copy.start()

    norm = 1.0 / math.sqrt(NW * NK)
    index_col = lax.broadcasted_iota(jnp.int32, (order, 128), 0)
    lane = lax.broadcasted_iota(jnp.int32, (order, 128), 1)
    freq = jnp.zeros((order, 128), jnp.int32)
    mom = jnp.zeros((order, 128), jnp.int32)
    for t in range(trans):
        start = shift_ref[t, 0]
        freq = jnp.where(lane == t, start // NK, freq)
        mom = jnp.where(lane == t, start % NK, mom)
    move = angle(move_steps(freq, mom, index_col))
    move_cos, move_sin = jnp.cos(move), jnp.sin(move)

    def put_cols(ref, t, real, imag):
        where = (slice(None),) if t is None else (t, slice(None))
        real, imag = (real * norm).astype(bf16), (imag * norm).astype(bf16)
        ref[where[:-1] + (slice(0, order), slice(0, order))] = real
        ref[where[:-1] + (slice(0, order), slice(order, 2 * order))] = -imag
        ref[where[:-1] + (slice(order, 2 * order), slice(0, order))] = imag
        ref[where[:-1] + (slice(order, 2 * order), slice(order, 2 * order))] = real

    site = lax.broadcasted_iota(jnp.int32, (order, order), 0)
    momentum = lax.broadcasted_iota(jnp.int32, (order, order), 1)
    phase = angle(base_steps(momentum, site))
    cos, sin = jnp.cos(phase), jnp.sin(phase)
    put_cols(col_table, None, cos, sin)
    for t in range(trans):
        mc, ms = move_cos[:, t : t + 1], move_sin[:, t : t + 1]
        cc, ss, sc, cs = mc * cos, ms * sin, ms * cos, mc * sin
        put_cols(sh_cols, t, cc - ss, sc + cs)
        put_cols(fl_cols, t, cc + ss, sc - cs)

    row = lax.broadcasted_iota(jnp.int32, (height, order), 0) + group * height
    column = lax.broadcasted_iota(jnp.int32, (height, order), 1)
    phase = angle(base_steps(row, column))
    cos, sin = jnp.cos(phase), jnp.sin(phase)
    band[0:height, :] = (cos * norm).astype(bf16)
    band[height : 2 * height, :] = (sin * norm).astype(bf16)
    col8 = lax.broadcasted_iota(jnp.int32, (8, order), 1)
    for t in range(trans):
        start = shift_ref[t, 0]
        move = angle(move_steps(start // NK, start % NK, col8))
        mc, ms = jnp.cos(move)[0:1], jnp.sin(move)[0:1]
        cc, ss, sc, cs = mc * cos, ms * sin, ms * cos, mc * sin
        first = 2 * t * height
        sh_rows[first : first + height, :] = ((cc - ss) * norm).astype(bf16)
        sh_rows[first + height : first + 2 * height, :] = ((sc + cs) * norm).astype(bf16)
        fl_rows[first : first + height, :] = ((cc + ss) * norm).astype(bf16)
        fl_rows[first + height : first + 2 * height, :] = ((sc - cs) * norm).astype(bf16)

    def dot(a, b):
        return jnp.dot(a, b, preferred_element_type=f32)

    def absorb(slot):
        for w in range(walkers):
            place = pl.ds(pl.multiple_of((slot * walkers + w) * height, height), height)
            signed = (2 * held_spins[slot, w : w + 1, :] - 1).astype(f32)
            lefts = []
            for s in range(2):
                factor = jnp.exp((COUPLING if s == 0 else -COUPLING) * signed)
                scaled = (held[slot, w, s].astype(f32) * factor).astype(bf16)
                moved = dot(sh_rows[...], scaled).astype(bf16)
                for t in range(trans):
                    first = 2 * t * height
                    x_ph[t, s, place, 0:order] = moved[first : first + height]
                    x_ph[t, s, place, order:] = moved[first + height : first + 2 * height]
                if s == 1:
                    moved = dot(fl_rows[...], scaled).astype(bf16)
                    for t in range(trans):
                        first = 2 * t * height
                        x_pp[t, place, 0:order] = moved[first : first + height]
                        x_pp[t, place, order:] = moved[first + height : first + 2 * height]
                else:
                    upper = dot(band[...], scaled).astype(bf16)
                left = lax.dot_general(band[...], scaled, NT, preferred_element_type=f32)
                lefts.append(left.astype(bf16))
            lefts.append(upper)
            joined = jnp.concatenate(
                [jnp.concatenate([one[:height], one[height:]], 1) for one in lefts], 0
            )
            second = dot(joined, col_table[...])
            for part in range(3):
                fixed[part, place, :] = second[part * height : (part + 1) * height]

    @pl.loop(0, reach + 3)
    def _(k):
        @pl.when(jnp.logical_and(k >= 1, k <= reach))
        def _():
            arrival(k, group).wait_recv()
            for step in range(1, chips):
                to_far(k, step).start()
            to_core(k).start()

        @pl.when(jnp.logical_and(k >= 2, k <= reach + 1))
        def _():
            for step in range(1, chips):
                arrival(k - 1, far(step)).wait_recv()
                relay(k - 1, step).start()

        @pl.when(k == 2)
        def _():
            local[0].wait()
            local[1].wait()

        @pl.when(k >= 3)
        def _():
            arrival(k - 2, partner).wait_recv()
            for step in range(1, chips):
                piece = lax.rem(chip + step, chips) * 2 + (1 - core)
                arrival(k - 2, piece).wait_recv()
            direct(k - 2)[1].wait_recv()

        @pl.when(k >= 2)
        def _():
            absorb(k - 2)

    local[2].wait()
    local[3].wait()
    length = (reach + 1) * walkers

    def product(left, right):
        for v in range(length):
            part = slice(v * height, (v + 1) * height)
            a, b = left[part, 0:order], left[part, order:]
            c, d = right[part, 0:order], right[part, order:]
            yield a, b, c, d

    @pl.loop(0, trans)
    def _(t):
        real, imag = ph_out[0, t], ph_out[1, t]
        for s in range(2):
            moved = dot(x_ph[t, s], sh_cols[t])
            for a, b, c, d in product(fixed[s], moved):
                real = real + (a * c + b * d)
                imag = imag + (a * d - b * c)
        ph_out[0, t] = real
        ph_out[1, t] = imag
        real, imag = pp_out[0, t], pp_out[1, t]
        lowered = dot(x_pp[t], fl_cols[t])
        for a, b, c, d in product(fixed[2], lowered):
            real = real + (a * c - b * d)
            imag = imag + (a * d + b * c)
        pp_out[0, t] = real
        pp_out[1, t] = imag

    for offset in range(1, reach + 1):
        for copy in direct(offset):
            copy.wait_send()
        to_core(offset).wait_send()
        for step in range(1, chips):
            to_far(offset, step).wait_send()
            relay(offset, step).wait_send()


def on_device(masses, spins, shift_table, flip_table, ph_in, pp_in):
    groups = lax.axis_size("grp")
    blocks = lax.axis_size("blk")
    reach = min(8, blocks - 1)
    visits = reach + 1
    walkers, _, order, _ = masses.shape
    trans = shift_table.shape[0]
    height = order // groups
    chips = groups // 2
    f32, bf16 = jnp.float32, jnp.bfloat16
    dma = pltpu.SemaphoreType.DMA
    anywhere = pl.BlockSpec(memory_space=pl.ANY)
    return pl.pallas_call(
        functools.partial(kernel, blocks, groups, reach),
        out_shape=(
            jax.ShapeDtypeStruct(ph_in.shape, f32),
            jax.ShapeDtypeStruct(pp_in.shape, f32),
        ),
        in_specs=[pl.BlockSpec(memory_space=pltpu.SMEM)] + [anywhere] * 4,
        out_specs=(pl.BlockSpec(memory_space=pltpu.VMEM),) * 2,
        scratch_shapes=[
            pltpu.VMEM((visits, walkers, 2, order, order), bf16),
            pltpu.VMEM((visits, walkers, order), jnp.int32),
            pltpu.VMEM((2 * order, 2 * order), bf16),
            pltpu.VMEM((trans, 2 * order, 2 * order), bf16),
            pltpu.VMEM((trans, 2 * order, 2 * order), bf16),
            pltpu.VMEM((2 * height, order), bf16),
            pltpu.VMEM((trans * 2 * height, order), bf16),
            pltpu.VMEM((trans * 2 * height, order), bf16),
            pltpu.VMEM((trans, 2, visits * walkers * height, 2 * order), bf16),
            pltpu.VMEM((trans, visits * walkers * height, 2 * order), bf16),
            pltpu.VMEM((3, visits * walkers * height, 2 * order), f32),
            dma((visits, groups)),
            dma((visits,)),
            dma((visits,)),
            dma((visits,)),
            dma((visits,)),
            dma((chips, visits)),
            dma((chips, visits)),
            dma((4,)),
        ],
        compiler_params=pltpu.CompilerParams(
            collective_id=0, has_side_effects=True, vmem_limit_bytes=56 * 1024 * 1024
        ),
    )(shift_table, masses, spins, ph_in, pp_in)


def solution(mesh):
    placed = (
        P("blk", None, None, None),
        P("blk", None),
        P("blk", None),
        P("blk", None),
        P(None, "blk", "grp", None),
        P(None, "blk", "grp", None),
    )
    return jax.shard_map(
        on_device,
        mesh=mesh,
        in_specs=placed,
        out_specs=(P(None, "blk", "grp", None), P(None, "blk", "grp", None)),
        check_vma=False,
    )
```

time: 1110 us -> 39.2 us (0.04); the launches traced: 1100 us -> 38.7 us
  other arithmetic: 544 us -> 0 us
  local copies, waits for them, and re-layouts: 366 us -> 2.72 us
  loops' own time: 171 us -> 0 us
  Pallas kernels: 0 us -> 35.3 us
    concatenate x116 -> x0, other arithmetic: 476 us -> none  [cyclic_window(): doubled = jnp.concatenate([grid, grid], axis)]
    dynamic_slice x128 -> x0, local copies, waits for them, and re-layouts: 220 us -> none  [the longest x64 182 us: cyclic_window(): return lax.dynamic_slice_in_dim(doubled, start, length, axis)]
    another operation x8 -> x0, loops' own time: 171 us -> none  [absorb(): ph_step, pp_step = lax.map(one_transfer, (shift_starts, flip_starts))]
    another operation x25 -> x0, local copies, waits for them, and re-layouts: 50.6 us -> none  [the longest x7 33 us: absorb(): view = propagator.reshape(2, 2, NW, NK, NW, NK)]
    pallas_call x0 -> x1, Pallas kernels: none -> 35.3 us  [on_device(): pl.pallas_call(functools.partial(kernel, blocks, groups, reach), out_shap...]
    convert_element_type x81 -> x0, other arithmetic: 35.1 us -> none  [the longest x32 19 us: one_transfer(): moved_band(view, shift_freq, shift_mom, first_freq, band_freq)]
    slice x113 -> x0, local copies, waits for them, and re-layouts: 33.8 us -> none  [the longest x96 18.7 us: one_transfer(): pp_real = upper[0] * lowered[0] - upper[1] * lowered[1]]
    rev x8 -> x0, local copies, waits for them, and re-layouts: 30.7 us -> none  [absorb(): reversed_lower = view[1, :, ::-1, ::-1, ::-1, ::-1]]
  transfers between devices with their start and end apart: 7 -> 0, of which waited for: 0 -> 0; matrix products, arithmetic and copies ran while one was open for 58% -> 0% of each run, Pallas kernels for 0% -> 0%
where the time goes in v1:
time: 39.2 us; the launch traced here: 38.7 us
  Pallas kernels  35.3 us (90%)
  local copies, waits for them, and re-layouts  2.72 us (7%)
  between operations  0.65 us (2%)
    pallas_call x1, Pallas kernels, on_device(): pl.pallas_call(functools.partial(kernel, blocks, groups, reach), out_shap...  35.3 us
    unnamed x4, local copies, waits for them, and re-layouts  2.72 us

profile of v1, /device:TPU:1, one launch (start us, length us, event | category | flops | bytes accessed | tf_op | source)
XLA Modules:
  0.0 38.7 jit_solution(14763246747077290299)
XLA Ops:
  0.6 35.3 %shard_map.68 = (f32[2,4,64,256]{3,2,1,0:T(8,128)}, f32[2,4,64,256]{3,2,1,0:T(8,128)}) custom-call(s32[4,256]{1,0:T(4,128)} %shift_ref.1, bf16[1,2,256,256]{3,2,1,0:T(8,128)(2,1)} %masses_ref.1, s32[1,256]{1,0:T(1,128)} %spins_ref.1, f32[2,4,64,256]{3,2,1,0:T(8,128)} %ph_ref.1, f32[2,4,64,256]{3,2,1,0:T(8,128)} %pp_ref.1), custom_call_target="tpu_custom_call" | custom-call | tf_op jit(solution)/shard_map/pallas_call | solution.py:284
  36.0 0.0 copy-start
  36.0 1.9 %copy.9 = f32[2,4,64,256]{3,2,1,0:T(8,128)} copy(f32[2,4,64,256]{3,2,1,0:T(8,128)} %get-tuple-element.4) | data formatting | bytes 1048576
  37.9 0.0 copy-done
  37.9 0.8 %copy.10 = f32[2,4,64,256]{3,2,1,0:T(8,128)} copy(f32[2,4,64,256]{3,2,1,0:T(8,128)S(1)} %copy-done) | data formatting | bytes 1048576
Async XLA Ops:
  36.0 1.9 %copy-start = (f32[2,4,64,256]{3,2,1,0:T(8,128)S(1)}, f32[2,4,64,256]{3,2,1,0:T(8,128)}, u32[]{:S(2)}) copy-start(f32[2,4,64,256]{3,2,1,0:T(8,128)} %get-tuple-element.5) | copy-start | bytes 1572868

commit v2 on v1

--- a/solution.py
+++ b/solution.py
@@ -11,6 +11,8 @@
 NW = 16
 NK = 16
 COUPLING = 0.5
+DIRECT = 6
+LAG = 2
 MESH = pl.DeviceIdType.MESH
 NT = (((1,), (1,)), ((), ()))
 
@@ -50,23 +52,58 @@
     def rows_of(piece):
         return pl.ds(pl.multiple_of(piece * height, height), height)
 
+    gather = reach + 1 == blocks and blocks % 2 == 0 and chips == 2
+    layers = blocks // 2
+    layer, side = block // 2, block % 2
+
+    def along(offset):
+        return lax.rem(layer + offset + layers, layers) * 2 + side
+
+    beside = layer * 2 + (1 - side)
+    half = order // 2
+    own_rows, far_rows = half * DIRECT // 8, half * (8 - DIRECT) // 8
+    own_first = core * half + chip * far_rows
+    give_first = core * half + chip * own_rows
+    take_first = core * half + (1 - chip) * own_rows
+    both_first = core * half + far_rows
+    both_rows = own_rows - far_rows
+    home = block if gather else 0
+    near = [sorted(set(range(layers)) - {one}, key=lambda z: abs(z - one)) for one in range(layers)]
+
+    def near_layer(rank):
+        found = 0
+        for one in range(layers):
+            for i in range(layers - 1):
+                hit = jnp.logical_and(layer == one, rank == i)
+                found = found + jnp.where(hit, near[one][i], 0)
+        return found
+
+    def source_of(step):
+        rank = lax.rem(step + layers - 2, layers - 1)
+        direct_side = jnp.where(step <= layers, side, 1 - side)
+        found = near_layer(rank) * 2 + direct_side
+        return jnp.where(step == 0, block, jnp.where(step == 1, beside, found))
+
     barrier = pltpu.get_barrier_semaphore()
-    for offset in range(1, reach + 1):
-        source = lax.rem(block - offset + blocks, blocks)
+    if gather:
+        sources = [along(offset) for offset in range(1, layers)] + [beside]
+    else:
+        sources = [lax.rem(block - offset + blocks, blocks) for offset in range(1, reach + 1)]
+    for source in sources:
         pl.semaphore_signal(barrier, inc=1, device_id=(group, source), device_id_type=MESH)
     pl.semaphore_signal(barrier, inc=1, device_id=(partner, block), device_id_type=MESH)
     for step in range(1, chips):
         pl.semaphore_signal(barrier, inc=1, device_id=(far(step), block), device_id_type=MESH)
 
     local = [
-        pltpu.make_async_copy(masses_ref, held.at[0], local_sem.at[0]),
-        pltpu.make_async_copy(spins_ref, held_spins.at[0], local_sem.at[1]),
+        pltpu.make_async_copy(masses_ref, held.at[home], local_sem.at[0]),
+        pltpu.make_async_copy(spins_ref, held_spins.at[home], local_sem.at[1]),
         pltpu.make_async_copy(ph_ref, ph_out, local_sem.at[2]),
         pltpu.make_async_copy(pp_ref, pp_out, local_sem.at[3]),
     ]
     for copy in local:
         copy.start()
-    pl.semaphore_wait(barrier, reach + chips)
+    pl.semaphore_wait(barrier, len(sources) + chips)
 
     def direct(offset):
         target = (group, lax.rem(block + offset, blocks))
@@ -74,7 +111,7 @@
             pltpu.make_async_remote_copy(
                 src_ref=masses_ref.at[:, :, rows_of(group)],
                 dst_ref=held.at[offset, :, :, rows_of(group)],
-                send_sem=direct_sem.at[offset],
+                send_sem=direct_sem.at[offset, 0],
                 recv_sem=recv_sem.at[offset, group],
                 device_id=target,
                 device_id_type=MESH,
@@ -82,7 +119,7 @@
             pltpu.make_async_remote_copy(
                 src_ref=spins_ref,
                 dst_ref=held_spins.at[offset],
-                send_sem=spin_send.at[offset],
+                send_sem=spin_send.at[offset, 0],
                 recv_sem=spin_recv.at[offset],
                 device_id=target,
                 device_id_type=MESH,
@@ -101,7 +138,7 @@
         )
 
     def to_core(offset):
-        return passed(offset, group, partner, core_sem.at[offset])
+        return passed(offset, group, partner, core_sem.at[offset, 0])
 
     def to_far(offset, step):
         return passed(offset, group, far(step), far_sem.at[step, offset])
@@ -110,11 +147,66 @@
         return passed(offset, far(step), partner, relay_sem.at[step, offset])
 
     def arrival(offset, piece):
-        return passed(offset, piece, partner, core_sem.at[offset])
-
-    for offset in range(1, reach + 1):
-        for copy in direct(offset):
+        return passed(offset, piece, partner, core_sem.at[offset, 0])
+
+    def send(src, dst, send_sem, recv, target):
+        return pltpu.make_async_remote_copy(
+            src_ref=src,
+            dst_ref=dst,
+            send_sem=send_sem,
+            recv_sem=recv,
+            device_id=target,
+            device_id_type=MESH,
+        )
+
+    def block_rows(slot, first, count):
+        return held.at[slot, :, :, pl.ds(pl.multiple_of(first, 16), count)]
+
+    def part_of(piece):
+        return ((give_first, far_rows), (both_first, both_rows))[piece]
+
+    def hop(slot, target, piece, own):
+        first, count = part_of(piece)
+        dst = block_rows(slot, first, count)
+        src = masses_ref.at[:, :, pl.ds(pl.multiple_of(first, 16), count)] if own else dst
+        return send(src, dst, direct_sem.at[slot if not own else target, piece + 2 * own],
+                    recv_sem.at[slot, piece], (group, target))
+
+    def note(slot, target, own):
+        return send(spins_ref if own else held_spins.at[slot], held_spins.at[slot],
+                    spin_send.at[slot if not own else target, 0 + own], spin_recv.at[slot],
+                    (group, target))
+
+    def own_hops():
+        targets = [beside] + [near_layer(i) * 2 + side for i in range(layers - 1)]
+        return [hop(block, target, 0, 1) for target in targets] + [
+            copy for target in targets
+            for copy in (note(block, target, 1), hop(block, target, 1, 1))
+        ]
+
+    def across(slot):
+        view = block_rows(slot, give_first, far_rows)
+        return send(view, view, far_sem.at[0, slot], recv_sem.at[slot, 2], (far(1), block))
+
+    def taken(slot):
+        view = block_rows(slot, take_first, far_rows)
+        return send(view, view, far_sem.at[0, slot], recv_sem.at[slot, 2], (far(1), block))
+
+    def share(slot):
+        view = block_rows(slot, own_first, own_rows)
+        return send(view, view, core_sem.at[slot, 0], recv_sem.at[slot, 3], (partner, block))
+
+    def share_taken(slot):
+        view = block_rows(slot, take_first, far_rows)
+        return send(view, view, core_sem.at[slot, 1], recv_sem.at[slot, 4], (partner, block))
+
+    if gather:
+        for copy in own_hops():
             copy.start()
+    else:
+        for offset in range(1, reach + 1):
+            for copy in direct(offset):
+                copy.start()
 
     norm = 1.0 / math.sqrt(NW * NK)
     index_col = lax.broadcasted_iota(jnp.int32, (order, 128), 0)
@@ -199,37 +291,83 @@
             for part in range(3):
                 fixed[part, place, :] = second[part * height : (part + 1) * height]
 
-    @pl.loop(0, reach + 3)
-    def _(k):
-        @pl.when(jnp.logical_and(k >= 1, k <= reach))
-        def _():
-            arrival(k, group).wait_recv()
-            for step in range(1, chips):
-                to_far(k, step).start()
-            to_core(k).start()
-
-        @pl.when(jnp.logical_and(k >= 2, k <= reach + 1))
-        def _():
-            for step in range(1, chips):
-                arrival(k - 1, far(step)).wait_recv()
-                relay(k - 1, step).start()
-
-        @pl.when(k == 2)
-        def _():
-            local[0].wait()
-            local[1].wait()
-
-        @pl.when(k >= 3)
-        def _():
-            arrival(k - 2, partner).wait_recv()
-            for step in range(1, chips):
-                piece = lax.rem(chip + step, chips) * 2 + (1 - core)
-                arrival(k - 2, piece).wait_recv()
-            direct(k - 2)[1].wait_recv()
-
-        @pl.when(k >= 2)
-        def _():
-            absorb(k - 2)
+    if gather:
+
+        @pl.loop(0, reach + LAG + 2)
+        def _(k):
+            @pl.when(jnp.logical_and(k >= 1, k <= reach))
+            def _():
+                slot = source_of(k)
+                hop(slot, beside, 0, 0).wait_recv()
+                across(slot).start()
+
+                @pl.when(jnp.logical_and(k >= 2, k <= layers))
+                def _():
+                    hop(slot, beside, 0, 0).start()
+
+            @pl.when(jnp.logical_and(k >= LAG + 1, k <= reach + LAG))
+            def _():
+                slot = source_of(k - LAG)
+                hop(slot, beside, 1, 0).wait_recv()
+                note(slot, beside, 0).wait_recv()
+
+                @pl.when(jnp.logical_and(k >= LAG + 2, k <= layers + LAG))
+                def _():
+                    hop(slot, beside, 1, 0).start()
+                    note(slot, beside, 0).start()
+
+                share(slot).start()
+                taken(slot).wait_recv()
+                share_taken(slot).start()
+
+            @pl.when(k == LAG + 1)
+            def _():
+                local[0].wait()
+                local[1].wait()
+
+            @pl.when(k >= LAG + 2)
+            def _():
+                slot = source_of(k - LAG - 1)
+                share(slot).wait_recv()
+                share_taken(slot).wait_recv()
+
+            @pl.when(k >= LAG + 1)
+            def _():
+                absorb(source_of(k - LAG - 1))
+
+    else:
+
+        @pl.loop(0, reach + 3)
+        def _(k):
+            @pl.when(jnp.logical_and(k >= 1, k <= reach))
+            def _():
+                arrival(k, group).wait_recv()
+                for step in range(1, chips):
+                    to_far(k, step).start()
+                to_core(k).start()
+
+            @pl.when(jnp.logical_and(k >= 2, k <= reach + 1))
+            def _():
+                for step in range(1, chips):
+                    arrival(k - 1, far(step)).wait_recv()
+                    relay(k - 1, step).start()
+
+            @pl.when(k == 2)
+            def _():
+                local[0].wait()
+                local[1].wait()
+
+            @pl.when(k >= 3)
+            def _():
+                arrival(k - 2, partner).wait_recv()
+                for step in range(1, chips):
+                    piece = lax.rem(chip + step, chips) * 2 + (1 - core)
+                    arrival(k - 2, piece).wait_recv()
+                direct(k - 2)[1].wait_recv()
+
+            @pl.when(k >= 2)
+            def _():
+                absorb(k - 2)
 
     local[2].wait()
     local[3].wait()
@@ -260,13 +398,26 @@
         pp_out[0, t] = real
         pp_out[1, t] = imag
 
-    for offset in range(1, reach + 1):
-        for copy in direct(offset):
+    if gather:
+        for copy in own_hops():
             copy.wait_send()
-        to_core(offset).wait_send()
-        for step in range(1, chips):
-            to_far(offset, step).wait_send()
-            relay(offset, step).wait_send()
+        for step in range(1, reach + 1):
+            slot = source_of(step)
+            if 2 <= step <= layers:
+                hop(slot, beside, 0, 0).wait_send()
+                hop(slot, beside, 1, 0).wait_send()
+                note(slot, beside, 0).wait_send()
+            across(slot).wait_send()
+            share(slot).wait_send()
+            share_taken(slot).wait_send()
+    else:
+        for offset in range(1, reach + 1):
+            for copy in direct(offset):
+                copy.wait_send()
+            to_core(offset).wait_send()
+            for step in range(1, chips):
+                to_far(offset, step).wait_send()
+                relay(offset, step).wait_send()
 
 
 def on_device(masses, spins, shift_table, flip_table, ph_in, pp_in):
@@ -301,11 +452,11 @@
             pltpu.VMEM((trans, 2, visits * walkers * height, 2 * order), bf16),
             pltpu.VMEM((trans, visits * walkers * height, 2 * order), bf16),
             pltpu.VMEM((3, visits * walkers * height, 2 * order), f32),
-            dma((visits, groups)),
+            dma((visits, max(groups, 5))),
             dma((visits,)),
-            dma((visits,)),
-            dma((visits,)),
-            dma((visits,)),
+            dma((visits, 4)),
+            dma((visits, 2)),
+            dma((visits, 2)),
             dma((chips, visits)),
             dma((chips, visits)),
             dma((4,)),

time: 39.2 us -> 33 us (0.84)
  Pallas kernels: 35.3 us -> 29.4 us
    pallas_call x1, Pallas kernels: 35.3 us -> 29.4 us  [on_device(): pl.pallas_call(functools.partial(kernel, blocks, groups, reach), out_shap...]
where the time goes in v2:
time: 33 us; the launch traced here: 32.8 us
  Pallas kernels  29.4 us (89%)
  local copies, waits for them, and re-layouts  2.72 us (8%)
  between operations  0.65 us (2%)
    pallas_call x1, Pallas kernels, on_device(): pl.pallas_call(functools.partial(kernel, blocks, groups, reach), out_shap...  29.4 us
    unnamed x4, local copies, waits for them, and re-layouts  2.72 us

profile of v2, /device:TPU:1, one launch (start us, length us, event | category | flops | bytes accessed | tf_op | source)
XLA Modules:
  0.0 32.8 jit_solution(365613470109211478)
XLA Ops:
  0.6 29.4 %shard_map.68 = (f32[2,4,64,256]{3,2,1,0:T(8,128)}, f32[2,4,64,256]{3,2,1,0:T(8,128)}) custom-call(s32[4,256]{1,0:T(4,128)} %shift_ref.1, bf16[1,2,256,256]{3,2,1,0:T(8,128)(2,1)} %masses_ref.1, s32[1,256]{1,0:T(1,128)} %spins_ref.1, f32[2,4,64,256]{3,2,1,0:T(8,128)} %ph_ref.1, f32[2,4,64,256]{3,2,1,0:T(8,128)} %pp_ref.1), custom_call_target="tpu_custom_call" | custom-call | tf_op jit(solution)/shard_map/pallas_call | solution.py:435
  30.1 0.0 copy-start
  30.1 1.9 %copy.9 = f32[2,4,64,256]{3,2,1,0:T(8,128)} copy(f32[2,4,64,256]{3,2,1,0:T(8,128)} %get-tuple-element.4) | data formatting | bytes 1048576
  32.0 0.0 copy-done
  32.0 0.8 %copy.10 = f32[2,4,64,256]{3,2,1,0:T(8,128)} copy(f32[2,4,64,256]{3,2,1,0:T(8,128)S(1)} %copy-done) | data formatting | bytes 1048576
Async XLA Ops:
  30.1 1.9 %copy-start = (f32[2,4,64,256]{3,2,1,0:T(8,128)S(1)}, f32[2,4,64,256]{3,2,1,0:T(8,128)}, u32[]{:S(2)}) copy-start(f32[2,4,64,256]{3,2,1,0:T(8,128)} %get-tuple-element.5) | copy-start | bytes 1572868

commit v3 on v2

--- a/solution.py
+++ b/solution.py
@@ -79,7 +79,7 @@
         return found
 
     def source_of(step):
-        rank = lax.rem(step + layers - 2, layers - 1)
+        rank = lax.rem(step + 2 * layers - 4, layers - 1)
         direct_side = jnp.where(step <= layers, side, 1 - side)
         found = near_layer(rank) * 2 + direct_side
         return jnp.where(step == 0, block, jnp.where(step == 1, beside, found))

time: 33 us -> 31.9 us (0.967)
  Pallas kernels: 29.4 us -> 28.4 us
    pallas_call x1, Pallas kernels: 29.4 us -> 28.4 us  [on_device(): pl.pallas_call(functools.partial(kernel, blocks, groups, reach), out_shap...]
where the time goes in v3:
time: 31.9 us; the launch traced here: 31.8 us
  Pallas kernels  28.4 us (89%)
  local copies, waits for them, and re-layouts  2.72 us (9%)
  between operations  0.65 us (2%)
    pallas_call x1, Pallas kernels, on_device(): pl.pallas_call(functools.partial(kernel, blocks, groups, reach), out_shap...  28.4 us
    unnamed x4, local copies, waits for them, and re-layouts  2.72 us

profile of v3, /device:TPU:1, one launch (start us, length us, event | category | flops | bytes accessed | tf_op | source)
XLA Modules:
  0.0 31.8 jit_solution(9787072367025975259)
XLA Ops:
  0.6 28.4 %shard_map.68 = (f32[2,4,64,256]{3,2,1,0:T(8,128)}, f32[2,4,64,256]{3,2,1,0:T(8,128)}) custom-call(s32[4,256]{1,0:T(4,128)} %shift_ref.1, bf16[1,2,256,256]{3,2,1,0:T(8,128)(2,1)} %masses_ref.1, s32[1,256]{1,0:T(1,128)} %spins_ref.1, f32[2,4,64,256]{3,2,1,0:T(8,128)} %ph_ref.1, f32[2,4,64,256]{3,2,1,0:T(8,128)} %pp_ref.1), custom_call_target="tpu_custom_call" | custom-call | tf_op jit(solution)/shard_map/pallas_call | solution.py:435
  29.0 0.0 copy-start
  29.0 1.9 %copy.9 = f32[2,4,64,256]{3,2,1,0:T(8,128)} copy(f32[2,4,64,256]{3,2,1,0:T(8,128)} %get-tuple-element.4) | data formatting | bytes 1048576
  31.0 0.0 copy-done
  31.0 0.8 %copy.10 = f32[2,4,64,256]{3,2,1,0:T(8,128)} copy(f32[2,4,64,256]{3,2,1,0:T(8,128)S(1)} %copy-done) | data formatting | bytes 1048576
Async XLA Ops:
  29.0 1.9 %copy-start = (f32[2,4,64,256]{3,2,1,0:T(8,128)S(1)}, f32[2,4,64,256]{3,2,1,0:T(8,128)}, u32[]{:S(2)}) copy-start(f32[2,4,64,256]{3,2,1,0:T(8,128)} %get-tuple-element.5) | copy-start | bytes 1572868
